TPU v7x, 256 devices: a whole 4x4x8 slice. The times are simulated.
256 devices in a mesh: section: 4 (over z_lo), dp: 64 (over x, y, z_hi, core).
Axes of the slice: x: 4, y: 4, z: 8 (z_hi: 2, z_lo: 4; z = z_hi * 4 + z_lo), core: 2. Of those that a mesh axis runs over, the one named last changes fastest.
Arguments:
- section_inputs: bfloat16 [4, 12544, 2048], P('section', 'dp'), may hold values from -16 to 16
- norm_gain: float32 [4, 2048], P('section'), may hold values from 0.25 to 1.75
- query_gain: float32 [4, 2048], P('section'), may hold values from -5 to 5
- key_gain: float32 [4, 2048], P('section'), may hold values from -5 to 5
- output_weight: bfloat16 [4, 2048, 2048], P('section', 'dp'), may hold values from -0.125 to 0.125
- full_sequence_gradient: bfloat16 [256, 196, 2048], P('dp'), may hold values from -6 to 6
- patch_order: int32 [256, 196], P('dp'), may hold values from 0 to 195, each once within a row
Outputs:
- input_grads: bfloat16 [4, 12544, 2048], P('section', 'dp')
- weight_grads: float32 [4, 2048, 2048], P('section', 'dp')
- gain_grads: float32 [4, 3, 2048], P('section')
Inputs may be any that keep to these rules, and one draw needn't show every extreme that they name: `patch_order`: each row holds every patch number once; the first 49 are the kept patches.
All inputs are finite; a program needn't handle non-finite values.
Results may differ from a plain program's by a relative error of at most 0.0057.
Values may be sent and summed in bfloat16 or wider, within the bound.
A program may use at most 128 MiB of HBM per device.

v0:
```python
import math
import jax
import jax.numpy as jnp
from jax import lax
from jax.sharding import PartitionSpec as P

HEADS = 16
KEPT = 49
PATCHES = 196
MICRO = 2
highest = lax.Precision.HIGHEST


def from_behind(block, axis, distance):
    devices = range(lax.axis_size(axis))
    route = [(i - distance, i) for i in devices if i - distance in devices]
    return lax.ppermute(block, axis, route)


def normalize(inputs):
    values = inputs.astype(jnp.float32)
    centred = values - jnp.mean(values, axis=-1, keepdims=True)
    variance = jnp.mean(centred * centred, axis=-1, keepdims=True)
    inverse = lax.rsqrt(variance + 1e-06)
    return (centred * inverse, inverse)


def attend_forward(normed, gain_row, query_row, key_row, heads):
    row_count, feature_width = normed.shape
    head_width = feature_width // heads
    split_shape = (row_count // KEPT, KEPT, heads, head_width)
    hidden = normed * gain_row
    queries = (hidden * query_row).reshape(split_shape)
    key_rows = (hidden * key_row).reshape(split_shape)
    value_rows = hidden.reshape(split_shape)
    attention_logits = jnp.einsum(
        "bqhd,bkhd->bhqk", queries, key_rows, precision=highest
    ) / math.sqrt(head_width)
    softmaxed = jax.nn.softmax(attention_logits, axis=-1)
    mixed = jnp.einsum("bhqk,bkhd->bqhd", softmaxed, value_rows, precision=highest)
    return (
        hidden,
        queries,
        key_rows,
        value_rows,
        softmaxed,
        mixed.reshape(row_count, feature_width).astype(jnp.bfloat16),
    )


def attend_backward(
    cotangent,
    back,
    normed,
    inverse,
    hidden,
    queries,
    key_rows,
    value_rows,
    softmaxed,
    gain_row,
    query_row,
    key_row,
):
    row_count, feature_width = back.shape
    head_width = queries.shape[-1]
    back_split = back.reshape(queries.shape)
    soft_grad = jnp.einsum("bqhd,bkhd->bhqk", back_split, value_rows, precision=highest)
    value_grad = jnp.einsum("bhqk,bqhd->bkhd", softmaxed, back_split, precision=highest).reshape(
        row_count, feature_width
    )
    score_grad = (
        softmaxed
        * (soft_grad - jnp.sum(soft_grad * softmaxed, axis=-1, keepdims=True))
        / math.sqrt(head_width)
    )
    query_grad = jnp.einsum("bhqk,bkhd->bqhd", score_grad, key_rows, precision=highest).reshape(
        row_count, feature_width
    )
    key_grad = jnp.einsum("bhqk,bqhd->bkhd", score_grad, queries, precision=highest).reshape(
        row_count, feature_width
    )
    hidden_grad = query_grad * query_row + key_grad * key_row + value_grad
    normed_grad = hidden_grad * gain_row
    first_mean = jnp.mean(normed_grad, axis=-1, keepdims=True)
    second_mean = jnp.mean(normed_grad * normed, axis=-1, keepdims=True)
    input_grad = (
        cotangent.astype(jnp.float32) + inverse * (normed_grad - first_mean - normed * second_mean)
    ).astype(jnp.bfloat16)
    sums = jnp.stack(
        [
            jnp.sum(hidden_grad * normed, axis=0),
            jnp.sum(query_grad * hidden, axis=0),
            jnp.sum(key_grad * hidden, axis=0),
        ]
    )
    return (input_grad, sums)


def shards(
    section_inputs,
    norm_gain,
    query_gain,
    key_gain,
    output_weight,
    full_sequence_gradient,
    patch_order,
):
    inputs = section_inputs[0]
    row_count, feature_width = inputs.shape
    image_count = row_count // KEPT
    section = lax.axis_index("section")
    sections = lax.axis_size("section")
    all_images = image_count * lax.axis_size("dp")
    gain_row = norm_gain[0]
    query_row = query_gain[0]
    key_row = key_gain[0]
    weight = lax.all_gather(output_weight[0], "dp", axis=0, tiled=True)
    normed, inverse = normalize(inputs)
    hidden, queries, key_rows, value_rows, softmaxed, mixed = attend_forward(
        normed, gain_row, query_row, key_row, HEADS
    )
    kept = patch_order[:, :KEPT]
    chosen_patches = (
        kept[:, :, None] == jnp.arange(PATCHES, dtype=jnp.int32)[None, None, :]
    ).astype(jnp.bfloat16)
    upper_bound = (
        jnp.einsum(
            "usn,unj->usj",
            chosen_patches,
            full_sequence_gradient,
            preferred_element_type=jnp.float32,
        )
        .astype(jnp.bfloat16)
        .reshape(row_count, feature_width)
    )
    per_unit = image_count // MICRO
    unit_rows = per_unit * KEPT
    unit_count = image_count // per_unit
    step_count = unit_count + sections - 1

    def take_rows(array, unit):
        return lax.dynamic_slice_in_dim(array, unit * unit_rows, unit_rows, 0)

    def take_images(array, unit):
        return lax.dynamic_slice_in_dim(array, unit * per_unit, per_unit, 0)

    def put_rows(array, piece, unit, valid):
        present_value = take_rows(array, unit)
        return lax.dynamic_update_slice_in_dim(
            array, jnp.where(valid, piece, present_value), unit * unit_rows, 0
        )

    def advance(step_index, carry):
        received, cotangents, input_grads, sums, running_weight = carry
        unit = step_index - (sections - 1 - section)
        valid = jnp.logical_and(unit >= 0, unit < unit_count)
        safe_unit = jnp.clip(unit, 0, unit_count - 1)
        cotangent = jnp.where(section == sections - 1, take_rows(upper_bound, safe_unit), received)
        back = lax.dot_general(
            cotangent, weight, (((1,), (1,)), ((), ())), preferred_element_type=jnp.float32
        )
        input_grad, partial_sums = attend_backward(
            cotangent,
            back,
            take_rows(normed, safe_unit),
            take_rows(inverse, safe_unit),
            take_rows(hidden, safe_unit),
            take_images(queries, safe_unit),
            take_images(key_rows, safe_unit),
            take_images(value_rows, safe_unit),
            take_images(softmaxed, safe_unit),
            gain_row,
            query_row,
            key_row,
        )
        cotangents = put_rows(cotangents, cotangent, safe_unit, valid)
        input_grads = put_rows(input_grads, input_grad, safe_unit, valid)
        sums = sums + jnp.where(valid, partial_sums, 0.0)
        received = from_behind(input_grad, "section", -1)
        return (received, cotangents, input_grads, sums, running_weight)

    weight_offset = jnp.zeros((1,), jnp.float32)
    start_carry = (
        jnp.zeros((unit_rows, feature_width), jnp.bfloat16),
        jnp.zeros_like(inputs),
        jnp.zeros_like(inputs),
        jnp.zeros((3, feature_width), jnp.float32),
        weight_offset,
    )
    final_carry = lax.fori_loop(0, step_count, advance, start_carry)
    cotangents = final_carry[1]
    input_grads = final_carry[2]
    gain_total = lax.psum(final_carry[3], "dp") / all_images
    weight_share = (
        lax.psum_scatter(
            lax.dot_general(
                mixed, cotangents, (((0,), (0,)), ((), ())), preferred_element_type=jnp.float32
            ),
            "dp",
            scatter_dimension=0,
            tiled=True,
        )
        / all_images
    )
    return (input_grads[None], weight_share[None], gain_total[None])


def solution(mesh):
    return jax.shard_map(
        shards,
        mesh=mesh,
        in_specs=(
            P("section", "dp", None),
            P("section", None),
            P("section", None),
            P("section", None),
            P("section", "dp", None),
            P("dp", None, None),
            P("dp", None),
        ),
        out_specs=(P("section", "dp", None), P("section", "dp", None), P("section", None, None)),
        check_vma=False,
    )
```

profile of v0, /device:TPU:96, one launch (start us, length us, event | category | flops | bytes accessed | tf_op | source)
XLA Modules:
  0.0 857.8 jit_solution(7415387619002725321)
XLA Ops:
  8.0 2.8 convert_element_type.46
  11.1 1.5 multiply_reduce_fusion.7
  12.7 4.7 fusion.17
  17.4 2.5 reshape.197
  21.4 1.7 copy.26
  23.3 1.8 copy.25
  25.1 1.8 copy.23
  26.9 4.0 multiply_reduce_fusion.6
  32.1 3.7 fusion.23
  37.1 2.2 broadcast_multiply_fusion.2
  39.3 82.6 %all-gather.3.cloned.1.call-done = bf16[1,2048,2048]{2,1,0:T(8,128)(2,1)} async-done(((bf16[1,32,2048]{2,1,0:T(8,128)(2,1)}), bf16[1,2048,2048]{2,1,0:T(8,128)(2,1)}) %all-gather.3.cloned.1.call-update) | async-done | bytes 8388624 | tf_op jit(solution)/shard_map/all_gather | solution.py:118
  124.6 193.8 %while.22 = (s32[]{:T(128)}, bf16[98,2048]{1,0:T(8,128)(2,1)}, bf16[196,2048]{1,0:T(8,128)(2,1)}, bf16[196,2048]{1,0:T(8,128)(2,1)}, f32[3,2048]{1,0:T(4,128)S(1...) while((s32[]{:T(128)}, bf16[98,2048]{1,0:T(8,128)(2,1)}, ...), condition=%wide.region_11.12_spmd.clone, body=%wide.region_4.11_spmd.clone.sunk | while | flops 1300798208 | bytes 88767504 | solution.py:191
  124.7 2.2 dynamic-slice_select_fusion.6
  126.9 6.1 fusion.47
  133.3 3.1 multiply_reduce_fusion.11
  136.4 1.7 convolution_bitcast_fusion.6
  138.1 1.8 convolution_bitcast_fusion.5
  142.0 2.0 multiply_reduce_fusion.12
  149.2 1.4 dynamic-slice_select_fusion.7
  150.6 5.7 collective-permute-start
  156.2 3.3 dynamic_update_slice.22
  159.5 3.3 dynamic_update_slice.23
  162.9 2.3 collective-permute-done
  165.3 2.2 dynamic-slice_select_fusion.6
  167.5 6.1 fusion.47
  173.8 3.1 multiply_reduce_fusion.11
  177.0 1.7 convolution_bitcast_fusion.6
  178.7 1.8 convolution_bitcast_fusion.5
  182.6 2.0 multiply_reduce_fusion.12
  191.1 5.3 collective-permute-start
  196.4 3.1 dynamic_update_slice.22
  199.6 3.1 dynamic_update_slice.23
  202.8 1.8 collective-permute-done
  204.7 2.2 dynamic-slice_select_fusion.6
  206.9 6.1 fusion.47
  213.2 3.1 multiply_reduce_fusion.11
  216.4 1.7 convolution_bitcast_fusion.6
  218.1 1.8 convolution_bitcast_fusion.5
  221.9 2.0 multiply_reduce_fusion.12
  230.5 5.3 collective-permute-start
  235.8 3.1 dynamic_update_slice.22
  238.9 3.1 dynamic_update_slice.23
  243.1 2.2 dynamic-slice_select_fusion.6
  245.3 6.1 fusion.47
  251.7 3.1 multiply_reduce_fusion.11
  254.8 1.7 convolution_bitcast_fusion.6
  256.5 1.8 convolution_bitcast_fusion.5
  260.4 2.0 multiply_reduce_fusion.12
  269.0 5.3 collective-permute-start
  274.2 3.1 dynamic_update_slice.22
  277.4 3.1 dynamic_update_slice.23
  280.8 2.2 dynamic-slice_select_fusion.6
  283.0 6.1 fusion.47
  289.3 3.1 multiply_reduce_fusion.11
  292.5 1.7 convolution_bitcast_fusion.6
  294.2 1.8 convolution_bitcast_fusion.5
  298.0 2.0 multiply_reduce_fusion.12
  306.6 5.3 collective-permute-start
  311.9 3.1 dynamic_update_slice.22
  315.0 3.1 dynamic_update_slice.23
  318.4 9.5 %fusion.30 = f32[2048,2048]{1,0:T(8,128)} fusion(bf16[196,2048]{1,0:T(8,128)(2,1)} %bitcast.137, bf16[196,2048]{1,0:T(8,128)(2,1)} %get-tuple-element.412), kind=kOutput, calls=%fused_computation.62 | convolution fusion | flops 1644167168 | bytes 18382848 | tf_op jit(solution)/shard_map/dot_general | solution.py:197
  328.0 425.0 %psum.7 = f32[3,2048]{1,0:T(4,128)S(1)} all-reduce(f32[3,2048]{1,0:T(4,128)S(1)} %get-tuple-element.413), channel_id=1, replica_groups=mesh['section'=4,'dp'=64] {'dp'}, use_global_device_ids=true, to_apply=%region_13.14 | all-reduce | flops 6144 | bytes 49152 | tf_op jit(solution)/shard_map/psum | solution.py:194
  753.7 95.6 %reduce-scatter.2.cloned.1.call-done = f32[32,2048]{1,0:T(8,128)} async-done(((f32[2048,2048]{1,0:T(8,128)}), f32[32,2048]{1,0:T(8,128)}) %reduce-scatter.2.cloned.1.call-update) | async-done | bytes 262160 | tf_op jit(solution)/shard_map/reduce_scatter | solution.py:196
  849.3 1.7 multiply_bitcast_fusion
  (204 shorter events, 53.1 us)
Async XLA Ops:
  7.2 5.5 copy-start
  7.2 114.7 %all-gather.3.cloned.1.call-start = ((), (), s32[]{:S(2)}) async-start(), calls=%async_computation.2 | async-start | bytes 8519680 | tf_op jit(solution)/shard_map/all_gather | solution.py:118
  7.9 841.4 %reduce-scatter.2.cloned.1.call-start = ((), (), s32[]{:S(2)}) async-start(), calls=%async_computation.1 | async-start | bytes 17039360 | tf_op jit(solution)/shard_map/reduce_scatter | solution.py:196
  8.0 2.8 copy-start.8
  8.0 4.7 slice-start
  17.4 2.5 copy-start.11
  20.2 0.7 copy-start.12
  20.2 0.7 copy-start.13
  21.4 1.8 copy-start.14
  35.9 1.3 copy-start.9
  133.2 3.1 copy-start.6
  136.4 1.7 copy-start.5
  144.6 1.6 copy-start.2
  146.1 1.4 copy-start.3
  146.1 1.9 copy-start.7
  148.0 1.1 copy-start.10
  148.7 7.5 copy-start.4
  150.6 14.7 %collective-permute-start = (bf16[98,2048]{1,0:T(8,128)(2,1)}, bf16[98,2048]{1,0:T(8,128)(2,1)}, u32[]{:S(2)}, u32[]{:S(2)}) collective-permute-start(bf16[98,2048]{1,0:T(8,128)(2,1)} %get-tuple-element.688), channel_id=1, source_target_pairs={{64,0},{128,64},{192,128},{65,1},{129,65},{193,129},{66,2},{130,66... | collective-permute-start | bytes 1204232 | tf_op jit(solution)/shard_map/while/body/eval_jaxpr/ppermute | solution.py:17
  173.8 3.1 copy-start.6
  177.0 1.7 copy-start.5
  185.1 1.6 copy-start.2
  186.7 1.4 copy-start.3
  186.7 1.9 copy-start.7
  188.6 1.1 copy-start.10
  189.3 7.2 copy-start.4
  191.1 13.4 %collective-permute-start = (bf16[98,2048]{1,0:T(8,128)(2,1)}, bf16[98,2048]{1,0:T(8,128)(2,1)}, u32[]{:S(2)}, u32[]{:S(2)}) collective-permute-start(bf16[98,2048]{1,0:T(8,128)(2,1)} %get-tuple-element.688), channel_id=1, source_target_pairs={{64,0},{128,64},{192,128},{65,1},{129,65},{193,129},{66,2},{130,66... | collective-permute-start | bytes 1204232 | tf_op jit(solution)/shard_map/while/body/eval_jaxpr/ppermute | solution.py:17
  213.2 3.1 copy-start.6
  216.4 1.7 copy-start.5
  224.5 1.6 copy-start.2
  226.1 1.4 copy-start.3
  226.1 1.9 copy-start.7
  228.0 1.1 copy-start.10
  228.6 7.2 copy-start.4
  230.5 12.6 %collective-permute-start = (bf16[98,2048]{1,0:T(8,128)(2,1)}, bf16[98,2048]{1,0:T(8,128)(2,1)}, u32[]{:S(2)}, u32[]{:S(2)}) collective-permute-start(bf16[98,2048]{1,0:T(8,128)(2,1)} %get-tuple-element.688), channel_id=1, source_target_pairs={{64,0},{128,64},{192,128},{65,1},{129,65},{193,129},{66,2},{130,66... | collective-permute-start | bytes 1204232 | tf_op jit(solution)/shard_map/while/body/eval_jaxpr/ppermute | solution.py:17
  251.7 3.1 copy-start.6
  254.8 1.7 copy-start.5
  263.0 1.6 copy-start.2
  264.5 1.4 copy-start.3
  264.6 1.9 copy-start.7
  266.5 1.1 copy-start.10
  267.1 7.2 copy-start.4
  269.0 11.7 %collective-permute-start = (bf16[98,2048]{1,0:T(8,128)(2,1)}, bf16[98,2048]{1,0:T(8,128)(2,1)}, u32[]{:S(2)}, u32[]{:S(2)}) collective-permute-start(bf16[98,2048]{1,0:T(8,128)(2,1)} %get-tuple-element.688), channel_id=1, source_target_pairs={{64,0},{128,64},{192,128},{65,1},{129,65},{193,129},{66,2},{130,66... | collective-permute-start | bytes 1204232 | tf_op jit(solution)/shard_map/while/body/eval_jaxpr/ppermute | solution.py:17
  289.3 3.1 copy-start.6
  292.5 1.7 copy-start.5
  300.6 1.6 copy-start.2
  302.2 1.4 copy-start.3
  302.2 1.9 copy-start.7
  304.1 1.1 copy-start.10
  304.7 7.2 copy-start.4
  306.6 11.6 %collective-permute-start = (bf16[98,2048]{1,0:T(8,128)(2,1)}, bf16[98,2048]{1,0:T(8,128)(2,1)}, u32[]{:S(2)}, u32[]{:S(2)}) collective-permute-start(bf16[98,2048]{1,0:T(8,128)(2,1)} %get-tuple-element.688), channel_id=1, source_target_pairs={{64,0},{128,64},{192,128},{65,1},{129,65},{193,129},{66,2},{130,66... | collective-permute-start | bytes 1204232 | tf_op jit(solution)/shard_map/while/body/eval_jaxpr/ppermute | solution.py:17
  328.0 523.0 %copy-start.1 = (bf16[4,196,2048]{2,0,1:T(4,128)(2,1)S(1)}, bf16[4,196,2048]{2,0,1:T(4,128)(2,1)}, u32[]{:S(2)}) copy-start(bf16[4,196,2048]{2,0,1:T(4,128)(2,1)} %param.14) | copy-start | bytes 9633796
Sparse Core Ops, SparseCore 0:
  11.5 110.3 all-gather.2
  328.1 521.1 reduce-scatter.1
where the time goes:
time: 860 us; the launch traced here: 858 us
  blocking collectives  425 us (49%)
  waiting for transfers between devices  184 us (21%)
  matrix products  95.3 us (11%)
  local copies, waits for them, and re-layouts  80 us (9%)
  other arithmetic  31.3 us (4%)
  starting transfers between devices  26.8 us (3%)
  between operations  14.2 us (2%)
    psum x1, blocking collectives, shards(): gain_total = lax.psum(final_carry[3], 'dp') / all_images  425 us
    reduce_scatter x1, waiting for transfers between devices, shards(): lax.psum_scatter(lax.dot_general(mixed, cotangents, (((0,), (0,)), ((), (...  95.6 us
    all_gather x1, waiting for transfers between devices, shards(): weight = lax.all_gather(output_weight[0], 'dp', axis=0, tiled=True)  82.6 us
    dynamic_update_slice x10, local copies, waits for them, and re-layouts, put_rows(): lax.dynamic_update_slice_in_dim(array, jnp.where(valid, piece, present_va...  31.8 us
    dot_general x5, matrix products, advance(): lax.dot_general(cotangent, weight, (((1,), (1,)), ((), ())), preferred_el...  30.5 us
    ppermute x5, starting transfers between devices, from_behind(): return lax.ppermute(block, axis, route)  26.7 us
    while x110, local copies, waits for them, and re-layouts  22.4 us
    select_n x10, other arithmetic, put_rows(): jnp.where(valid, piece, present_value)  17.9 us
  transfers between devices with their start and end apart: 7, of which 6 were waited for; matrix products, arithmetic and copies ran while one was open for 7% of the time, Pallas kernels for 0%

commit v1 on v0

--- a/solution.py
+++ b/solution.py
@@ -191,7 +191,7 @@
     final_carry = lax.fori_loop(0, step_count, advance, start_carry)
     cotangents = final_carry[1]
     input_grads = final_carry[2]
-    gain_total = lax.psum(final_carry[3], "dp") / all_images
+    gain_total = jnp.sum(lax.all_gather(final_carry[3], "dp"), axis=0) / all_images
     weight_share = (
         lax.psum_scatter(
             lax.dot_general(

time: 860 us -> 924 us (1.074)
  waiting for transfers between devices: 184 us -> 669 us
  blocking collectives: 425 us -> 0 us
    psum x1 -> x0, blocking collectives: 425 us -> none  [shards(): gain_total = lax.psum(final_carry[3], 'dp') / all_images]
    reduce_scatter x1, waiting for transfers between devices: 95.6 us -> 514 us  [shards(): lax.psum_scatter(lax.dot_general(mixed, cotangents, (((0,), (0,)), ((), (...]
    all_gather x0 -> x1, waiting for transfers between devices: none -> 62.4 us  [shards(): lax.all_gather(final_carry[3], 'dp')]
  transfers between devices with their start and end apart: 7 -> 8, of which waited for: 6 -> 7; matrix products, arithmetic and copies ran while one was open for 7% -> 8% of each run, Pallas kernels for 0% -> 0%
where the time goes in v1:
time: 924 us; the launch traced here: 922 us
  waiting for transfers between devices  669 us (72%)
  matrix products  96.5 us (10%)
  local copies, waits for them, and re-layouts  80.6 us (9%)
  other arithmetic  33.1 us (4%)
  starting transfers between devices  27 us (3%)
  between operations  13.9 us (2%)
    reduce_scatter x1, waiting for transfers between devices, shards(): lax.psum_scatter(lax.dot_general(mixed, cotangents, (((0,), (0,)), ((), (...  514 us
    all_gather x1, waiting for transfers between devices, shards(): weight = lax.all_gather(output_weight[0], 'dp', axis=0, tiled=True)  87.1 us
    all_gather x1, waiting for transfers between devices, shards(): lax.all_gather(final_carry[3], 'dp')  62.4 us
    dynamic_update_slice x10, local copies, waits for them, and re-layouts, put_rows(): lax.dynamic_update_slice_in_dim(array, jnp.where(valid, piece, present_va...  31.8 us
    dot_general x5, matrix products, advance(): lax.dot_general(cotangent, weight, (((1,), (1,)), ((), ())), preferred_el...  30.5 us
    ppermute x5, starting transfers between devices, from_behind(): return lax.ppermute(block, axis, route)  26.9 us
    while x110, local copies, waits for them, and re-layouts  22.4 us
  transfers between devices with their start and end apart: 8, of which 7 were waited for; matrix products, arithmetic and copies ran while one was open for 8% of the time, Pallas kernels for 0%

profile of v1, /device:TPU:96, one launch (start us, length us, event | category | flops | bytes accessed | tf_op | source)
XLA Modules:
  0.0 921.6 jit_solution(7106424424973978805)
XLA Ops:
  8.0 2.7 convert_element_type.46
  11.0 1.5 multiply_reduce_fusion.7
  12.6 4.7 fusion.17
  17.4 2.4 reshape.206
  21.3 1.7 copy.41
  23.2 1.8 copy.40
  25.0 1.8 copy.38
  26.9 4.0 multiply_reduce_fusion.6
  32.6 2.2 broadcast_multiply_fusion.2
  34.8 87.1 %all-gather.6.cloned.1.call-done = bf16[1,2048,2048]{2,1,0:T(8,128)(2,1)} async-done(((bf16[1,32,2048]{2,1,0:T(8,128)(2,1)}), bf16[1,2048,2048]{2,1,0:T(8,128)(2,1)}) %all-gather.6.cloned.1.call-update) | async-done | bytes 8388624 | tf_op jit(solution)/shard_map/all_gather | solution.py:118
  124.6 194.2 %while.22 = (s32[]{:T(128)}, bf16[98,2048]{1,0:T(8,128)(2,1)}, bf16[196,2048]{1,0:T(8,128)(2,1)}, bf16[196,2048]{1,0:T(8,128)(2,1)}, f32[3,2048]{1,0:T(4,128)S(1...) while((s32[]{:T(128)}, bf16[98,2048]{1,0:T(8,128)(2,1)}, ...), condition=%wide.region_11.12_spmd.clone, body=%wide.region_4.11_spmd.clone.sunk | while | flops 1300798208 | bytes 88767504 | solution.py:191
  124.7 2.2 dynamic-slice_select_fusion.6
  126.9 6.1 fusion.47
  133.2 3.1 multiply_reduce_fusion.11
  136.4 1.7 convolution_bitcast_fusion.6
  138.1 1.8 convolution_bitcast_fusion.5
  142.0 2.0 multiply_reduce_fusion.12
  150.6 5.7 collective-permute-start
  156.3 3.3 dynamic_update_slice.22
  159.6 3.3 dynamic_update_slice.23
  163.0 2.3 collective-permute-done
  165.4 2.2 dynamic-slice_select_fusion.6
  167.6 6.1 fusion.47
  173.9 3.1 multiply_reduce_fusion.11
  177.1 1.7 convolution_bitcast_fusion.6
  178.8 1.8 convolution_bitcast_fusion.5
  182.7 2.0 multiply_reduce_fusion.12
  191.2 5.3 collective-permute-start
  196.6 3.1 dynamic_update_slice.22
  199.7 3.1 dynamic_update_slice.23
  202.9 1.8 collective-permute-done
  204.8 2.2 dynamic-slice_select_fusion.6
  207.0 6.1 fusion.47
  213.4 3.1 multiply_reduce_fusion.11
  216.5 1.7 convolution_bitcast_fusion.6
  218.2 1.8 convolution_bitcast_fusion.5
  222.1 2.0 multiply_reduce_fusion.12
  230.7 5.3 collective-permute-start
  236.0 3.1 dynamic_update_slice.22
  239.1 3.1 dynamic_update_slice.23
  243.4 2.2 dynamic-slice_select_fusion.6
  245.6 6.1 fusion.47
  251.9 3.2 multiply_reduce_fusion.11
  255.1 1.7 convolution_bitcast_fusion.6
  256.8 1.8 convolution_bitcast_fusion.5
  260.7 2.0 multiply_reduce_fusion.12
  269.3 5.3 collective-permute-start
  274.6 3.1 dynamic_update_slice.22
  277.7 3.1 dynamic_update_slice.23
  281.1 2.2 dynamic-slice_select_fusion.6
  283.3 6.1 fusion.47
  289.6 3.2 multiply_reduce_fusion.11
  292.8 1.7 convolution_bitcast_fusion.6
  294.5 1.8 convolution_bitcast_fusion.5
  298.4 2.0 multiply_reduce_fusion.12
  307.0 5.3 collective-permute-start
  312.3 3.1 dynamic_update_slice.22
  315.4 3.1 dynamic_update_slice.23
  319.5 5.1 fusion.23
  325.1 9.3 %fusion.30 = f32[2048,2048]{1,0:T(8,128)} fusion(bf16[196,2048]{1,0:T(8,128)(2,1)S(1)} %bitcast.138, bf16[196,2048]{1,0:T(8,128)(2,1)} %get-tuple-element.412), kind=kOutput, calls=%fused_computation.62 | convolution fusion | flops 1644167168 | bytes 18382848 | tf_op jit(solution)/shard_map/dot_general | solution.py:197
  334.4 62.4 %all-gather.8.cloned.1.call-done = f32[64,3,2048]{2,1,0:T(4,128)} async-done(((f32[1,3,2048]{2,1,0:T(4,128)}), f32[64,3,2048]{2,1,0:T(4,128)}) %all-gather.8.cloned.1.call-update) | async-done | bytes 1572880 | tf_op jit(solution)/shard_map/all_gather | solution.py:194
  396.8 1.9 reduce_sum.125
  399.4 514.0 %reduce-scatter.2.cloned.1.call-done = f32[32,2048]{1,0:T(8,128)} async-done(((f32[2048,2048]{1,0:T(8,128)}), f32[32,2048]{1,0:T(8,128)}) %reduce-scatter.2.cloned.1.call-update) | async-done | bytes 262160 | tf_op jit(solution)/shard_map/reduce_scatter | solution.py:196
  913.3 1.7 multiply_bitcast_fusion
  (211 shorter events, 55.0 us)
Async XLA Ops:
  7.2 5.5 copy-start
  7.2 114.6 %all-gather.6.cloned.1.call-start = ((), (), s32[]{:S(2)}) async-start(), calls=%async_computation.2 | async-start | bytes 8519680 | tf_op jit(solution)/shard_map/all_gather | solution.py:118
  7.9 388.9 %all-gather.8.cloned.1.call-start = ((), (), s32[]{:S(2)}) async-start(), calls=%async_computation.3 | async-start | bytes 2129920 | tf_op jit(solution)/shard_map/all_gather | solution.py:194
  8.0 2.8 copy-start.9
  8.0 4.6 slice-start
  17.4 2.4 copy-start.12
  20.1 0.7 copy-start.13
  20.1 0.7 copy-start.15
  21.3 1.9 copy-start.5
  21.3 1.8 copy-start.16
  31.4 1.1 copy-start.10
  133.2 3.1 copy-start.7
  136.4 1.7 copy-start.6
  144.6 1.6 copy-start.2
  146.1 1.4 copy-start.3
  146.1 1.9 copy-start.8
  148.1 1.1 copy-start.11
  148.7 7.6 copy-start.4
  150.6 14.7 %collective-permute-start = (bf16[98,2048]{1,0:T(8,128)(2,1)}, bf16[98,2048]{1,0:T(8,128)(2,1)}, u32[]{:S(2)}, u32[]{:S(2)}) collective-permute-start(bf16[98,2048]{1,0:T(8,128)(2,1)} %get-tuple-element.707), channel_id=1, source_target_pairs={{64,0},{128,64},{192,128},{65,1},{129,65},{193,129},{66,2},{130,66... | collective-permute-start | bytes 1204232 | tf_op jit(solution)/shard_map/while/body/eval_jaxpr/ppermute | solution.py:17
  173.9 3.1 copy-start.7
  177.0 1.7 copy-start.6
  185.2 1.6 copy-start.2
  186.8 1.4 copy-start.3
  186.8 1.9 copy-start.8
  188.7 1.1 copy-start.11
  189.4 7.2 copy-start.4
  191.2 13.5 %collective-permute-start = (bf16[98,2048]{1,0:T(8,128)(2,1)}, bf16[98,2048]{1,0:T(8,128)(2,1)}, u32[]{:S(2)}, u32[]{:S(2)}) collective-permute-start(bf16[98,2048]{1,0:T(8,128)(2,1)} %get-tuple-element.707), channel_id=1, source_target_pairs={{64,0},{128,64},{192,128},{65,1},{129,65},{193,129},{66,2},{130,66... | collective-permute-start | bytes 1204232 | tf_op jit(solution)/shard_map/while/body/eval_jaxpr/ppermute | solution.py:17
  213.3 3.1 copy-start.7
  216.5 1.7 copy-start.6
  224.7 1.6 copy-start.2
  226.2 1.4 copy-start.3
  226.3 1.9 copy-start.8
  228.2 1.1 copy-start.11
  228.8 7.2 copy-start.4
  230.7 12.6 %collective-permute-start = (bf16[98,2048]{1,0:T(8,128)(2,1)}, bf16[98,2048]{1,0:T(8,128)(2,1)}, u32[]{:S(2)}, u32[]{:S(2)}) collective-permute-start(bf16[98,2048]{1,0:T(8,128)(2,1)} %get-tuple-element.707), channel_id=1, source_target_pairs={{64,0},{128,64},{192,128},{65,1},{129,65},{193,129},{66,2},{130,66... | collective-permute-start | bytes 1204232 | tf_op jit(solution)/shard_map/while/body/eval_jaxpr/ppermute | solution.py:17
  251.9 3.2 copy-start.7
  255.1 1.7 copy-start.6
  263.3 1.6 copy-start.2
  264.8 1.4 copy-start.3
  264.9 1.9 copy-start.8
  266.8 1.1 copy-start.11
  267.4 7.2 copy-start.4
  269.3 11.7 %collective-permute-start = (bf16[98,2048]{1,0:T(8,128)(2,1)}, bf16[98,2048]{1,0:T(8,128)(2,1)}, u32[]{:S(2)}, u32[]{:S(2)}) collective-permute-start(bf16[98,2048]{1,0:T(8,128)(2,1)} %get-tuple-element.707), channel_id=1, source_target_pairs={{64,0},{128,64},{192,128},{65,1},{129,65},{193,129},{66,2},{130,66... | collective-permute-start | bytes 1204232 | tf_op jit(solution)/shard_map/while/body/eval_jaxpr/ppermute | solution.py:17
  289.6 3.2 copy-start.7
  292.8 1.7 copy-start.6
  301.0 1.6 copy-start.2
  302.5 1.4 copy-start.3
  302.6 1.9 copy-start.8
  304.5 1.1 copy-start.11
  305.1 7.2 copy-start.4
  307.0 11.6 %collective-permute-start = (bf16[98,2048]{1,0:T(8,128)(2,1)}, bf16[98,2048]{1,0:T(8,128)(2,1)}, u32[]{:S(2)}, u32[]{:S(2)}) collective-permute-start(bf16[98,2048]{1,0:T(8,128)(2,1)} %get-tuple-element.707), channel_id=1, source_target_pairs={{64,0},{128,64},{192,128},{65,1},{129,65},{193,129},{66,2},{130,66... | collective-permute-start | bytes 1204232 | tf_op jit(solution)/shard_map/while/body/eval_jaxpr/ppermute | solution.py:17
  318.8 0.6 copy-start.14
  319.5 593.9 %reduce-scatter.2.cloned.1.call-start = ((), (), s32[]{:S(2)}) async-start(), calls=%async_computation.1 | async-start | bytes 17039360 | tf_op jit(solution)/shard_map/reduce_scatter | solution.py:196
  334.4 580.6 %copy-start.1 = (bf16[4,196,2048]{2,0,1:T(4,128)(2,1)S(1)}, bf16[4,196,2048]{2,0,1:T(4,128)(2,1)}, u32[]{:S(2)}) copy-start(bf16[4,196,2048]{2,0,1:T(4,128)(2,1)} %param.14) | copy-start | bytes 9633796
Sparse Core Ops, SparseCore 0:
  11.5 110.3 all-gather.5
  319.6 77.1 all-gather.7
  399.4 513.9 reduce-scatter.1
